TPU v7x, 32 devices: a whole 2x2x4 slice. The times are simulated.
32 devices in a mesh: groups: 2 (over y), tile: 4 (over z), col: 2 (over x), rep: 2 (over core).
Axes of the slice: x: 2, y: 2, z: 4, core: 2. Of those that a mesh axis runs over, the one named last changes fastest.
Arguments:
- forcing: bfloat16 [4, 20, 32, 2048], P(('groups', 'rep'), 'tile', None, 'col'), parts along dimension 0, may hold values from -6 to 6
- member_kernel_weight: bfloat16 [20, 576, 64], P('tile'), may hold values from -0.25 to 0.25
- member_counts: int32 [4], P('tile'), may hold values from 1 to 5, 16 in all
- mixing_input_weight: bfloat16 [1280, 512], P('tile'), may hold values from -0.1875 to 0.1875
- depth_weight: float32 [9, 512], replicated, may hold values from -2 to 2
- mix_weight: bfloat16 [512, 512], replicated, may hold values from -0.25 to 0.25
- cotangent: bfloat16 [4, 32, 32, 512], P(('groups', 'rep'), 'tile', 'col'), parts along dimension 0, may hold values from -6 to 6
Outputs:
- adjusted: bfloat16 [4, 32, 32, 512], P(('groups', 'rep'), 'tile', 'col'), parts along dimension 0
- mix_grad: float32 [1024, 512], P(('groups', 'tile', 'col', 'rep')), parts along dimension 0
- depth_grad: float32 [18, 512], P('groups'), parts along dimension 0
- in_grad: float32 [2560, 512], P(('groups', 'tile')), parts along dimension 0
- group_grad: float32 [40, 576, 64], P(('groups', 'tile')), parts along dimension 0
There are 2 independent parts, one for each index of `groups`. A program takes and returns all parts, laid end to end along the dimension named above; an argument that names none is the same for every part. Nothing has to cross between parts.
Inputs may be any that keep to these rules, and one draw needn't show every extreme that they name: member_counts sums to 16; each index of tile holds at least one member and at least one holds 5.
All inputs are finite; a program needn't handle non-finite values. No bound on the sum of `member_counts` on one device may be relied on, other than what follows from the above.
Results may differ from a plain program's by a relative error of at most 0.011.
Values may be sent and summed in bfloat16 or wider, within the bound.
No kernel may reach another device: no remote copies, remote signals or barrier semaphores. Data moves between devices by JAX's collectives and lax.ppermute only.
A program may use at most 64 MiB of HBM per device.

v0:
```python
import jax
import jax.numpy as jnp
from jax import lax
from jax.sharding import PartitionSpec as P


def extended_2(block, sides, width):
    for axis, dim in sides:
        count = lax.axis_size(axis)
        forward = [(i, i + 1) for i in range(count - 1)]
        backward = [(target, source) for source, target in forward]
        low = lax.ppermute(
            lax.slice_in_dim(block, block.shape[dim] - width, None, axis=dim), axis, forward
        )
        high = lax.ppermute(lax.slice_in_dim(block, 0, width, axis=dim), axis, backward)
        block = jnp.concatenate([low, block, high], axis=dim)
    return block


def silu_slope(value):
    sig = jax.nn.sigmoid(value)
    return sig * (1.0 + value * (1.0 - sig))


def slot_patches(extended, slot, channels):
    height = extended.shape[1]
    width = extended.shape[2] // channels - 2
    field = lax.dynamic_index_in_dim(extended, slot, 0, keepdims=False).reshape(
        height, width + 2, channels
    )
    padded = jnp.pad(field, ((1, 1), (0, 0), (0, 0)))
    stacked = jnp.concatenate(
        [
            padded[down : down + height, across : across + width]
            for down in range(3)
            for across in range(3)
        ],
        axis=-1,
    )
    return stacked.reshape(height * width, 9 * channels)


def fetch_weight(mixing_input_weight):
    full_weight = lax.all_gather(mixing_input_weight, "tile", axis=0, tiled=True)
    return full_weight


def local(
    forcing,
    member_kernel_weight,
    member_counts,
    mixing_input_weight,
    depth_weight,
    mix_weight,
    cotangent,
):
    channels = member_kernel_weight.shape[2]
    slots_here = forcing.shape[1]
    height = forcing.shape[2]
    width = forcing.shape[3] // channels
    hidden_width = mixing_input_weight.shape[1]
    slot_width = slots_here * channels
    count = member_counts[0]
    band = height // lax.axis_size("tile")
    extended = extended_2(forcing, (("col", 3),), channels)[0]

    def forward_slot(slot, buffer):
        columns = slot_patches(extended, slot, channels)
        weight = lax.dynamic_index_in_dim(member_kernel_weight, slot, 0, keepdims=False)
        gate = jnp.dot(columns, weight, preferred_element_type=jnp.float32)
        result = jax.nn.silu(gate).astype(jnp.bfloat16).reshape(height, width, channels)
        return lax.dynamic_update_slice_in_dim(buffer, result, slot * channels, 2)

    feature_maps = lax.fori_loop(
        0, count, forward_slot, jnp.zeros((height, width, slot_width), jnp.bfloat16)
    )
    full_weight = None
    gathered = lax.all_to_all(feature_maps, "tile", split_axis=0, concat_axis=2, tiled=True)
    all_width = gathered.shape[2]
    full_weight = fetch_weight(mixing_input_weight)
    mixed_in = jnp.dot(
        gathered.reshape(-1, all_width), full_weight, preferred_element_type=jnp.float32
    )
    mixed_in = mixed_in.astype(jnp.bfloat16).reshape(band, width, hidden_width)
    act_pad = extended_2(mixed_in, (("tile", 0), ("col", 1)), 1)
    before = jnp.zeros((band, width, hidden_width), jnp.float32)
    for down in range(3):
        for across in range(3):
            before = before + depth_weight[down * 3 + across] * act_pad[
                down : down + band, across : across + width
            ].astype(jnp.float32)
    hidden = jax.nn.silu(before).astype(jnp.bfloat16)
    flat_hidden = hidden.reshape(-1, hidden_width)
    adjusted = jnp.dot(flat_hidden, mix_weight.T, preferred_element_type=jnp.float32).astype(
        jnp.bfloat16
    )
    adjusted = adjusted.reshape(1, band, width, hidden_width)
    upstream = cotangent[0].reshape(-1, hidden_width)
    hidden_grad = jnp.dot(upstream, mix_weight, preferred_element_type=jnp.float32).reshape(
        band, width, hidden_width
    )
    before_grad = (hidden_grad * silu_slope(before)).astype(jnp.bfloat16)
    mix_grad = lax.psum_scatter(
        jnp.dot(upstream.T, flat_hidden, preferred_element_type=jnp.float32),
        ("tile", "col", "rep"),
        scatter_dimension=0,
        tiled=True,
    )
    grad_wide = before_grad.astype(jnp.float32)
    depth_terms = jnp.stack(
        [
            jnp.sum(
                act_pad[down : down + band, across : across + width].astype(jnp.float32)
                * grad_wide,
                axis=(0, 1),
            )
            for down in range(3)
            for across in range(3)
        ],
        axis=0,
    )
    depth_grad = lax.psum(depth_terms, ("tile", "col", "rep"))
    grad_pad = extended_2(before_grad, (("tile", 0), ("col", 1)), 1)
    act_grad = jnp.zeros((band, width, hidden_width), jnp.float32)
    for down in range(3):
        for across in range(3):
            act_grad = act_grad + depth_weight[down * 3 + across] * grad_pad[
                2 - down : 2 - down + band, 2 - across : 2 - across + width
            ].astype(jnp.float32)
    act_grad = act_grad.astype(jnp.bfloat16)
    piece = lax.all_gather(act_grad, "tile", axis=0, tiled=True)
    number = piece.shape[0]
    flat_piece = piece.reshape(-1, hidden_width)
    rows_here = feature_maps.reshape(-1, slot_width)
    weight_total = jnp.dot(rows_here.T, flat_piece, preferred_element_type=jnp.float32)
    block = jnp.dot(flat_piece, mixing_input_weight.T, preferred_element_type=jnp.float32).astype(
        jnp.bfloat16
    )
    buffer = block.reshape(number, width, slot_width)
    feature_gradient = buffer
    in_grad = lax.psum(weight_total.astype(jnp.bfloat16), ("col", "rep")).astype(jnp.float32)

    def backward_slot(slot, totals):
        columns = slot_patches(extended, slot, channels)
        weight = lax.dynamic_index_in_dim(member_kernel_weight, slot, 0, keepdims=False)
        gate = jnp.dot(columns, weight, preferred_element_type=jnp.float32)
        slot_grad = lax.dynamic_slice_in_dim(
            feature_gradient, slot * channels, channels, 2
        ).reshape(-1, channels)
        inner = (slot_grad.astype(jnp.float32) * silu_slope(gate)).astype(jnp.bfloat16)
        term = jnp.dot(columns.T, inner, preferred_element_type=jnp.float32)
        return lax.dynamic_update_index_in_dim(totals, term, slot, 0)

    group_term = lax.fori_loop(
        0, count, backward_slot, jnp.zeros((slots_here, 9 * channels, channels), jnp.float32)
    )
    group_grad = lax.psum(group_term.astype(jnp.bfloat16), ("col", "rep")).astype(jnp.float32)
    return (adjusted, mix_grad, depth_grad, in_grad, group_grad)


def solution(mesh):
    in_specs = (
        P(("groups", "rep"), "tile", None, "col"),
        P("tile", None, None),
        P("tile"),
        P("tile", None),
        P(),
        P(),
        P(("groups", "rep"), "tile", "col", None),
    )
    out_specs = (
        P(("groups", "rep"), "tile", "col", None),
        P(("groups", "tile", "col", "rep"), None),
        P("groups", None),
        P(("groups", "tile"), None),
        P(("groups", "tile"), None, None),
    )
    return jax.shard_map(local, mesh=mesh, in_specs=in_specs, out_specs=out_specs, check_vma=False)
```

profile of v0, /device:TPU:0, one launch (start us, length us, event | category | flops | bytes accessed | tf_op | source)
XLA Modules:
  0.0 233.5 jit_solution(2599027453419804770)
XLA Ops:
  8.2 4.9 %collective-permute-start = (bf16[1,5,32,64]{3,2,1,0:T(8,128)(2,1)S(1)}, bf16[1,5,32,64]{3,2,1,0:T(8,128)(2,1)S(1)}, u32[]{:S(2)}, u32[]{:S(2)}) collective-permute-start(bf16[1,5,32,64]{3,2,1,0:T(8,128)(2,1)S(1)} %get-tuple-element.229), channel_id=1, source_target_pairs={{0,2},{1,3},{4,6},{5,7},{8,10},{9,11},{12,14},{13,15},{16,18},{17,... | collective-permute-start | bytes 61448 | tf_op jit(solution)/shard_map/ppermute | solution.py:12
  14.7 4.2 %collective-permute-done.1 = bf16[1,5,32,64]{3,2,1,0:T(8,128)(2,1)S(1)} collective-permute-done((bf16[1,5,32,64]{3,2,1,0:T(8,128)(2,1)S(1)}, bf16[1,5,32,64]{3,2,1,0:T(8,128)(2,1)S(1)}, u32[]{:S(2)}, u32[]{:S(2)}) %collective-permute-start.1) | collective-permute-done | bytes 20512 | tf_op jit(solution)/shard_map/ppermute | solution.py:15
  20.3 27.4 %while.24 = (s32[]{:T(128)}, bf16[32,16,320]{2,1,0:T(8,128)(2,1)S(1)}, s32[]{:T(128)}, bf16[5,32,1152]{2,1,0:T(8,128)(2,1)S(1)}, bf16[5,576,64]{1,2,0:T(8,128)(2...) while((s32[]{:T(128)}, bf16[32,16,320]{2,1,0:T(8,128)(2,1)S(1)}, s32[]{:T(128)}, ...), condition=%wide.region_1.2_spmd, body=%wide.region_0.1_spmd.sunk | while | flops 37912580 | bytes 3653833 | solution.py:74
  26.8 5.0 %dynamic_update_slice.16 = bf16[32,16,320]{2,1,0:T(8,128)(2,1)S(1)} dynamic-update-slice(bf16[32,16,320]{2,1,0:T(8,128)(2,1)S(1)} %get-tuple-element.369, bf16[32,16,64]{2,1,0:T(8,128)(2,1)S(1)} %bitcast.109, s32[]{:T(128)} %constant.90.clone.1..sunk, s32[]{:T(128)} %constant.90.clone.1..sunk, s32[]{:T(128)S(6)} %select_n.35) | dynamic-update-slice | bytes 131076 | tf_op jit(solution)/shard_map/while/body/dynamic_update_slice | solution.py:72
  38.5 5.0 %dynamic_update_slice.16 = bf16[32,16,320]{2,1,0:T(8,128)(2,1)S(1)} dynamic-update-slice(bf16[32,16,320]{2,1,0:T(8,128)(2,1)S(1)} %get-tuple-element.369, bf16[32,16,64]{2,1,0:T(8,128)(2,1)S(1)} %bitcast.109, s32[]{:T(128)} %constant.90.clone.1..sunk, s32[]{:T(128)} %constant.90.clone.1..sunk, s32[]{:T(128)S(6)} %select_n.35) | dynamic-update-slice | bytes 131076 | tf_op jit(solution)/shard_map/while/body/dynamic_update_slice | solution.py:72
  47.7 12.9 %all_to_all.15 = bf16[32,16,320]{2,1,0:T(8,128)(2,1)S(1)} all-to-all(bf16[32,16,320]{2,1,0:T(8,128)(2,1)S(1)} %get-tuple-element.153), channel_id=1, replica_groups=mesh['groups'=2,'tile'=4,'col'=2,'rep'=2] {'tile'}, dimensions={0} | all-to-all | bytes 655360 | tf_op jit(solution)/shard_map/all_to_all | solution.py:78
  61.3 1.7 convolution_convert_fusion.2
  64.4 4.5 %collective-permute-start.2 = (bf16[1,16,512]{2,1,0:T(8,128)(2,1)S(1)}, bf16[1,16,512]{2,1,0:T(8,128)(2,1)S(1)}, u32[]{:S(2)}, u32[]{:S(2)}) collective-permute-start(bf16[1,16,512]{2,1,0:T(8,128)(2,1)S(1)} %get-tuple-element.240), channel_id=1, source_target_pairs={{0,4},{4,8},{8,12},{1,5},{5,9},{9,13},{2,6},{6,10},{10,14},{3,7},{... | collective-permute-start | bytes 49160 | tf_op jit(solution)/shard_map/ppermute | solution.py:12
  70.4 1.9 collective-permute-start.4
  73.8 4.2 %collective-permute-done.5 = bf16[10,1,512]{2,1,0:T(2,128)(2,1)S(1)} collective-permute-done((bf16[10,1,512]{2,1,0:T(2,128)(2,1)S(1)}, bf16[10,1,512]{2,1,0:T(2,128)(2,1)S(1)}, u32[]{:S(2)}, u32[]{:S(2)}) %collective-permute-start.5) | collective-permute-done | bytes 10272 | tf_op jit(solution)/shard_map/ppermute | solution.py:15
  81.5 4.8 %collective-permute-start.6 = (bf16[1,16,512]{2,1,0:T(8,128)(2,1)S(1)}, bf16[1,16,512]{2,1,0:T(8,128)(2,1)S(1)}, u32[]{:S(2)}, u32[]{:S(2)}) collective-permute-start(bf16[1,16,512]{2,1,0:T(8,128)(2,1)S(1)} %get-tuple-element.238), channel_id=1, source_target_pairs={{0,4},{4,8},{8,12},{1,5},{5,9},{9,13},{2,6},{6,10},{10,14},{3,7},{... | collective-permute-start | bytes 49160 | tf_op jit(solution)/shard_map/ppermute | solution.py:12
  89.1 4.5 %collective-permute-start.9 = (bf16[10,1,512]{2,1,0:T(2,128)(2,1)S(1)}, bf16[10,1,512]{2,1,0:T(2,128)(2,1)S(1)}, u32[]{:S(2)}, u32[]{:S(2)}) collective-permute-start(bf16[10,1,512]{2,1,0:T(2,128)(2,1)S(1)} %get-tuple-element.233), channel_id=1, source_target_pairs={{0,2},{1,3},{4,6},{5,7},{8,10},{9,11},{12,14},{13,15},{16,18},{17,... | collective-permute-start | bytes 30728 | tf_op jit(solution)/shard_map/ppermute | solution.py:12
  93.7 1.5 collective-permute-done.9
  95.5 16.0 %all_gather.7 = bf16[32,16,512]{2,1,0:T(8,128)(2,1)S(1)} all-gather(bf16[8,16,512]{2,1,0:T(8,128)(2,1)S(1)} %fusion.44), channel_id=1, replica_groups=mesh['groups'=2,'tile'=4,'col'=2,'rep'=2] {'tile'}, dimensions={0}, use_global_device_ids=true | all-gather | bytes 655360 | tf_op jit(solution)/shard_map/all_gather | solution.py:131
  113.2 16.9 %while.25 = (s32[]{:T(128)}, bf16[5,576,64]{1,2,0:T(8,128)(2,1)S(1)}, s32[]{:T(128)}, bf16[5,32,1152]{2,1,0:T(8,128)(2,1)S(1)}, bf16[32,16,320]{2,1,0:T(8,128)(2...) while((s32[]{:T(128)}, ...), condition=%wide.region_15.16_spmd, body=%wide.region_14.15_spmd.sunk | while | flops 75825160 | bytes 4932813 | solution.py:154
  115.1 1.4 fusion.74
  118.3 1.4 fusion.74
  121.6 1.4 fusion.74
  124.8 1.4 fusion.74
  128.1 1.4 fusion.74
  133.8 58.4 %psum.21 = f32[9,512]{1,0:T(8,128)} all-reduce(f32[9,512]{1,0:T(8,128)S(1)} %stack.39), channel_id=1, replica_groups=mesh['groups'=2,'tile'=4,'col'=2,'rep'=2] {'tile','col','rep'}, use_global_device_ids=true, to_apply=%region_12.13 | all-reduce | flops 4608 | bytes 36864 | tf_op jit(solution)/shard_map/psum | solution.py:122
  193.1 1.9 convert_element_type.146
  195.0 1.9 convert_element_type.149
  196.9 30.0 %reduce-scatter.4.cloned.1.call-done = f32[32,512]{1,0:T(8,128)} async-done(((f32[512,512]{1,0:T(8,128)}), f32[32,512]{1,0:T(8,128)}) %reduce-scatter.4.cloned.1.call-update) | async-done | bytes 65552
  (129 shorter events, 40.2 us)
Async XLA Ops:
  7.2 71.9 %copy-start = (bf16[512,512]{1,0:T(8,128)(2,1)S(1)}, bf16[512,512]{1,0:T(8,128)(2,1)}, u32[]{:S(2)}) copy-start(bf16[512,512]{1,0:T(8,128)(2,1)} %param.16) | copy-start | bytes 1572868
  7.2 54.1 %all-gather.2.cloned.1.call-start = ((), (), s32[]{:S(2)}) async-start(), calls=%async_computation.2 | async-start | bytes 1638400 | tf_op jit(solution)/shard_map/all_gather | solution.py:44
  8.2 6.5 %collective-permute-start = (bf16[1,5,32,64]{3,2,1,0:T(8,128)(2,1)S(1)}, bf16[1,5,32,64]{3,2,1,0:T(8,128)(2,1)S(1)}, u32[]{:S(2)}, u32[]{:S(2)}) collective-permute-start(bf16[1,5,32,64]{3,2,1,0:T(8,128)(2,1)S(1)} %get-tuple-element.229), channel_id=1, source_target_pairs={{0,2},{1,3},{4,6},{5,7},{8,10},{9,11},{12,14},{13,15},{16,18},{17,... | collective-permute-start | bytes 61448 | tf_op jit(solution)/shard_map/ppermute | solution.py:12
  13.0 5.9 %collective-permute-start.1 = (bf16[1,5,32,64]{3,2,1,0:T(8,128)(2,1)S(1)}, bf16[1,5,32,64]{3,2,1,0:T(8,128)(2,1)S(1)}, u32[]{:S(2)}, u32[]{:S(2)}) collective-permute-start(bf16[1,5,32,64]{3,2,1,0:T(8,128)(2,1)S(1)} %get-tuple-element.228), channel_id=1, source_target_pairs={{2,0},{3,1},{6,4},{7,5},{10,8},{11,9},{14,12},{15,13},{18,16},{19,... | collective-permute-start | bytes 61448 | tf_op jit(solution)/shard_map/ppermute | solution.py:15
  14.4 178.7 %all-reduce.5.cloned.1.call-start = ((), (), s32[]{:S(2)}) async-start(), calls=%async_computation.4 | async-start | bytes 1474560 | tf_op jit(solution)/shard_map/psum | solution.py:141
  60.9 12.7 %copy-start.5 = (f32[9,512]{1,0:T(8,128)S(1)}, f32[9,512]{1,0:T(8,128)}, u32[]{:S(2)}) copy-start(f32[9,512]{1,0:T(8,128)} %param.15) | copy-start | bytes 55300
  63.0 16.1 %copy-start.4 = (bf16[1,8,16,512]{3,2,1,0:T(8,128)(2,1)S(1)}, bf16[1,8,16,512]{3,2,1,0:T(8,128)(2,1)}, u32[]{:S(2)}) copy-start(bf16[1,8,16,512]{3,2,1,0:T(8,128)(2,1)} %param.17) | copy-start | bytes 393220
  63.0 6.0 %collective-permute-start.3 = (bf16[1,16,512]{2,1,0:T(8,128)(2,1)S(1)}, bf16[1,16,512]{2,1,0:T(8,128)(2,1)S(1)}, u32[]{:S(2)}, u32[]{:S(2)}) collective-permute-start(bf16[1,16,512]{2,1,0:T(8,128)(2,1)S(1)} %get-tuple-element.241), channel_id=1, source_target_pairs={{4,0},{8,4},{12,8},{5,1},{9,5},{13,9},{6,2},{10,6},{14,10},{7,3},{... | collective-permute-start | bytes 49160 | tf_op jit(solution)/shard_map/ppermute | solution.py:15
  64.4 6.0 %collective-permute-start.2 = (bf16[1,16,512]{2,1,0:T(8,128)(2,1)S(1)}, bf16[1,16,512]{2,1,0:T(8,128)(2,1)S(1)}, u32[]{:S(2)}, u32[]{:S(2)}) collective-permute-start(bf16[1,16,512]{2,1,0:T(8,128)(2,1)S(1)} %get-tuple-element.240), channel_id=1, source_target_pairs={{0,4},{4,8},{8,12},{1,5},{5,9},{9,13},{2,6},{6,10},{10,14},{3,7},{... | collective-permute-start | bytes 49160 | tf_op jit(solution)/shard_map/ppermute | solution.py:12
  70.4 3.4 %collective-permute-start.4 = (bf16[10,1,512]{2,1,0:T(2,128)(2,1)S(1)}, bf16[10,1,512]{2,1,0:T(2,128)(2,1)S(1)}, u32[]{:S(2)}, u32[]{:S(2)}) collective-permute-start(bf16[10,1,512]{2,1,0:T(2,128)(2,1)S(1)} %get-tuple-element.236), channel_id=1, source_target_pairs={{0,2},{1,3},{4,6},{5,7},{8,10},{9,11},{12,14},{13,15},{16,18},{17,... | collective-permute-start | bytes 30728 | tf_op jit(solution)/shard_map/ppermute | solution.py:12
  72.4 5.7 %collective-permute-start.5 = (bf16[10,1,512]{2,1,0:T(2,128)(2,1)S(1)}, bf16[10,1,512]{2,1,0:T(2,128)(2,1)S(1)}, u32[]{:S(2)}, u32[]{:S(2)}) collective-permute-start(bf16[10,1,512]{2,1,0:T(2,128)(2,1)S(1)} %get-tuple-element.237), channel_id=1, source_target_pairs={{2,0},{3,1},{6,4},{7,5},{10,8},{11,9},{14,12},{15,13},{18,16},{19,... | collective-permute-start | bytes 30728 | tf_op jit(solution)/shard_map/ppermute | solution.py:15
  80.2 6.1 %collective-permute-start.7 = (bf16[1,16,512]{2,1,0:T(8,128)(2,1)S(1)}, bf16[1,16,512]{2,1,0:T(8,128)(2,1)S(1)}, u32[]{:S(2)}, u32[]{:S(2)}) collective-permute-start(bf16[1,16,512]{2,1,0:T(8,128)(2,1)S(1)} %get-tuple-element.239), channel_id=1, source_target_pairs={{4,0},{8,4},{12,8},{5,1},{9,5},{13,9},{6,2},{10,6},{14,10},{7,3},{... | collective-permute-start | bytes 49160 | tf_op jit(solution)/shard_map/ppermute | solution.py:15
  81.5 6.3 %collective-permute-start.6 = (bf16[1,16,512]{2,1,0:T(8,128)(2,1)S(1)}, bf16[1,16,512]{2,1,0:T(8,128)(2,1)S(1)}, u32[]{:S(2)}, u32[]{:S(2)}) collective-permute-start(bf16[1,16,512]{2,1,0:T(8,128)(2,1)S(1)} %get-tuple-element.238), channel_id=1, source_target_pairs={{0,4},{4,8},{8,12},{1,5},{5,9},{9,13},{2,6},{6,10},{10,14},{3,7},{... | collective-permute-start | bytes 49160 | tf_op jit(solution)/shard_map/ppermute | solution.py:12
  87.8 5.9 %collective-permute-start.8 = (bf16[10,1,512]{2,1,0:T(2,128)(2,1)S(1)}, bf16[10,1,512]{2,1,0:T(2,128)(2,1)S(1)}, u32[]{:S(2)}, u32[]{:S(2)}) collective-permute-start(bf16[10,1,512]{2,1,0:T(2,128)(2,1)S(1)} %get-tuple-element.232), channel_id=1, source_target_pairs={{2,0},{3,1},{6,4},{7,5},{10,8},{11,9},{14,12},{15,13},{18,16},{19,... | collective-permute-start | bytes 30728 | tf_op jit(solution)/shard_map/ppermute | solution.py:15
  89.1 6.0 %collective-permute-start.9 = (bf16[10,1,512]{2,1,0:T(2,128)(2,1)S(1)}, bf16[10,1,512]{2,1,0:T(2,128)(2,1)S(1)}, u32[]{:S(2)}, u32[]{:S(2)}) collective-permute-start(bf16[10,1,512]{2,1,0:T(2,128)(2,1)S(1)} %get-tuple-element.233), channel_id=1, source_target_pairs={{0,2},{1,3},{4,6},{5,7},{8,10},{9,11},{12,14},{13,15},{16,18},{17,... | collective-permute-start | bytes 30728 | tf_op jit(solution)/shard_map/ppermute | solution.py:12
  111.5 1.1 copy-start.2
  130.2 0.8 copy-start.1
  131.0 96.0 %reduce-scatter.4.cloned.1.call-start = ((), (), s32[]{:S(2)}) async-start(), calls=%async_computation.3 | async-start | bytes 1114112
  132.3 1.4 copy-start.6
  132.3 1.4 copy-start.7
  132.3 1.4 copy-start.8
  132.3 59.8 %copy-start.3 = (bf16[8,16,512]{2,1,0:T(8,128)(2,1)S(1)}, bf16[8,16,512]{2,1,0:T(8,128)(2,1)}, u32[]{:S(2)}) copy-start(bf16[8,16,512]{2,1,0:T(8,128)(2,1)} %get-tuple-element.208) | copy-start | bytes 393220
Sparse Core Ops, SparseCore 0:
  14.5 34.9 all-gather.1
  131.1 33.7 all-reduce.4
  169.0 57.8 reduce-scatter.3
where the time goes:
time: 235 us; the launch traced here: 233 us
  blocking collectives  87.3 us (37%)
  waiting for transfers between devices  43.2 us (18%)
  local copies, waits for them, and re-layouts  27.7 us (12%)
  starting transfers between devices  27.4 us (12%)
  matrix products  19.9 us (8%)
  between operations  14.1 us (6%)
  loops' own time  8.51 us (4%)
  other arithmetic  5.39 us (2%)
    psum x1, blocking collectives, local(): depth_grad = lax.psum(depth_terms, ('tile', 'col', 'rep'))  58.4 us
    unnamed x4, waiting for transfers between devices  30.1 us
    ppermute x5, starting transfers between devices, extended_2(): lax.ppermute(lax.slice_in_dim(block, block.shape[dim] - width, None, axis...  20.7 us
    all_gather x1, blocking collectives, local(): piece = lax.all_gather(act_grad, 'tile', axis=0, tiled=True)  16 us
    all_to_all x1, blocking collectives, local(): lax.all_to_all(feature_maps, 'tile', split_axis=0, concat_axis=2, tiled=T...  12.9 us
    dynamic_update_slice x5, local copies, waits for them, and re-layouts, forward_slot(): return lax.dynamic_update_slice_in_dim(buffer, result, slot * channels, 2)  12.2 us
    ppermute x5, waiting for transfers between devices, extended_2(): lax.ppermute(lax.slice_in_dim(block, 0, width, axis=dim), axis, backward)  8.46 us
    dot_general x5, matrix products, backward_slot(): term = jnp.dot(columns.T, inner, preferred_element_type=jnp.float32)  7.15 us
  transfers between devices with their start and end apart: 13, of which 8 were waited for; matrix products, arithmetic and copies ran while one was open for 14% of the time, Pallas kernels for 0%

commit v1 on v0

--- a/solution.py
+++ b/solution.py
@@ -119,7 +119,8 @@
         ],
         axis=0,
     )
-    depth_grad = lax.psum(depth_terms, ("tile", "col", "rep"))
+    terms = lax.all_gather(depth_terms, ("tile", "col", "rep"))
+    depth_grad = jnp.sum(terms, axis=0)
     grad_pad = extended_2(before_grad, (("tile", 0), ("col", 1)), 1)
     act_grad = jnp.zeros((band, width, hidden_width), jnp.float32)
     for down in range(3):

time: 235 us -> 236 us (level)
  waiting for transfers between devices: 43.2 us -> 81.9 us
  blocking collectives: 87.3 us -> 49.8 us
    psum x1 -> x0, blocking collectives: 58.4 us -> none  [local(): depth_grad = lax.psum(depth_terms, ('tile', 'col', 'rep'))]
    unnamed x4, waiting for transfers between devices: 30.1 us -> 58.3 us
    all_gather x0 -> x1, blocking collectives: none -> 20.8 us  [local(): terms = lax.all_gather(depth_terms, ('tile', 'col', 'rep'))]
    psum x1, waiting for transfers between devices: 0.01 us -> 10.5 us  [local(): lax.psum(weight_total.astype(jnp.bfloat16), ('col', 'rep'))]
  transfers between devices with their start and end apart: 13 -> 13, of which waited for: 8 -> 9; matrix products, arithmetic and copies ran while one was open for 14% -> 14% of each run, Pallas kernels for 0% -> 0%
where the time goes in v1:
time: 236 us; the launch traced here: 235 us
  waiting for transfers between devices  81.9 us (35%)
  blocking collectives  49.8 us (21%)
  local copies, waits for them, and re-layouts  27.7 us (12%)
  starting transfers between devices  27.4 us (12%)
  matrix products  19.9 us (8%)
  between operations  14.1 us (6%)
  loops' own time  8.51 us (4%)
  other arithmetic  6.04 us (3%)
    unnamed x4, waiting for transfers between devices  58.3 us
    all_gather x1, blocking collectives, local(): terms = lax.all_gather(depth_terms, ('tile', 'col', 'rep'))  20.8 us
    ppermute x5, starting transfers between devices, extended_2(): lax.ppermute(lax.slice_in_dim(block, block.shape[dim] - width, None, axis...  20.7 us
    all_gather x1, blocking collectives, local(): piece = lax.all_gather(act_grad, 'tile', axis=0, tiled=True)  16 us
    all_to_all x1, blocking collectives, local(): lax.all_to_all(feature_maps, 'tile', split_axis=0, concat_axis=2, tiled=T...  12.9 us
    dynamic_update_slice x5, local copies, waits for them, and re-layouts, forward_slot(): return lax.dynamic_update_slice_in_dim(buffer, result, slot * channels, 2)  12.2 us
    psum x1, waiting for transfers between devices, local(): lax.psum(weight_total.astype(jnp.bfloat16), ('col', 'rep'))  10.5 us
    ppermute x5, waiting for transfers between devices, extended_2(): lax.ppermute(lax.slice_in_dim(block, 0, width, axis=dim), axis, backward)  8.46 us
  transfers between devices with their start and end apart: 13, of which 9 were waited for; matrix products, arithmetic and copies ran while one was open for 14% of the time, Pallas kernels for 0%

profile of v1, /device:TPU:0, one launch (start us, length us, event | category | flops | bytes accessed | tf_op | source)
XLA Modules:
  0.0 235.2 jit_solution(18017784891626273623)
XLA Ops:
  8.2 4.9 %collective-permute-start = (bf16[1,5,32,64]{3,2,1,0:T(8,128)(2,1)S(1)}, bf16[1,5,32,64]{3,2,1,0:T(8,128)(2,1)S(1)}, u32[]{:S(2)}, u32[]{:S(2)}) collective-permute-start(bf16[1,5,32,64]{3,2,1,0:T(8,128)(2,1)S(1)} %get-tuple-element.229), channel_id=1, source_target_pairs={{0,2},{1,3},{4,6},{5,7},{8,10},{9,11},{12,14},{13,15},{16,18},{17,... | collective-permute-start | bytes 61448 | tf_op jit(solution)/shard_map/ppermute | solution.py:12
  14.7 4.2 %collective-permute-done.1 = bf16[1,5,32,64]{3,2,1,0:T(8,128)(2,1)S(1)} collective-permute-done((bf16[1,5,32,64]{3,2,1,0:T(8,128)(2,1)S(1)}, bf16[1,5,32,64]{3,2,1,0:T(8,128)(2,1)S(1)}, u32[]{:S(2)}, u32[]{:S(2)}) %collective-permute-start.1) | collective-permute-done | bytes 20512 | tf_op jit(solution)/shard_map/ppermute | solution.py:15
  20.3 27.4 %while.24 = (s32[]{:T(128)}, bf16[32,16,320]{2,1,0:T(8,128)(2,1)S(1)}, s32[]{:T(128)}, bf16[5,32,1152]{2,1,0:T(8,128)(2,1)S(1)}, bf16[5,576,64]{1,2,0:T(8,128)(2...) while((s32[]{:T(128)}, bf16[32,16,320]{2,1,0:T(8,128)(2,1)S(1)}, s32[]{:T(128)}, ...), condition=%wide.region_1.2_spmd, body=%wide.region_0.1_spmd.sunk | while | flops 37912580 | bytes 3653833 | solution.py:74
  26.8 5.0 %dynamic_update_slice.16 = bf16[32,16,320]{2,1,0:T(8,128)(2,1)S(1)} dynamic-update-slice(bf16[32,16,320]{2,1,0:T(8,128)(2,1)S(1)} %get-tuple-element.369, bf16[32,16,64]{2,1,0:T(8,128)(2,1)S(1)} %bitcast.110, s32[]{:T(128)} %constant.90.clone.1..sunk, s32[]{:T(128)} %constant.90.clone.1..sunk, s32[]{:T(128)S(6)} %select_n.35) | dynamic-update-slice | bytes 131076 | tf_op jit(solution)/shard_map/while/body/dynamic_update_slice | solution.py:72
  38.5 5.0 %dynamic_update_slice.16 = bf16[32,16,320]{2,1,0:T(8,128)(2,1)S(1)} dynamic-update-slice(bf16[32,16,320]{2,1,0:T(8,128)(2,1)S(1)} %get-tuple-element.369, bf16[32,16,64]{2,1,0:T(8,128)(2,1)S(1)} %bitcast.110, s32[]{:T(128)} %constant.90.clone.1..sunk, s32[]{:T(128)} %constant.90.clone.1..sunk, s32[]{:T(128)S(6)} %select_n.35) | dynamic-update-slice | bytes 131076 | tf_op jit(solution)/shard_map/while/body/dynamic_update_slice | solution.py:72
  47.7 12.9 %all_to_all.15 = bf16[32,16,320]{2,1,0:T(8,128)(2,1)S(1)} all-to-all(bf16[32,16,320]{2,1,0:T(8,128)(2,1)S(1)} %get-tuple-element.153), channel_id=1, replica_groups=mesh['groups'=2,'tile'=4,'col'=2,'rep'=2] {'tile'}, dimensions={0} | all-to-all | bytes 655360 | tf_op jit(solution)/shard_map/all_to_all | solution.py:78
  61.3 1.7 convolution_convert_fusion.2
  64.4 4.5 %collective-permute-start.2 = (bf16[1,16,512]{2,1,0:T(8,128)(2,1)S(1)}, bf16[1,16,512]{2,1,0:T(8,128)(2,1)S(1)}, u32[]{:S(2)}, u32[]{:S(2)}) collective-permute-start(bf16[1,16,512]{2,1,0:T(8,128)(2,1)S(1)} %get-tuple-element.240), channel_id=1, source_target_pairs={{0,4},{4,8},{8,12},{1,5},{5,9},{9,13},{2,6},{6,10},{10,14},{3,7},{... | collective-permute-start | bytes 49160 | tf_op jit(solution)/shard_map/ppermute | solution.py:12
  70.4 1.9 collective-permute-start.4
  73.8 4.2 %collective-permute-done.5 = bf16[10,1,512]{2,1,0:T(2,128)(2,1)S(1)} collective-permute-done((bf16[10,1,512]{2,1,0:T(2,128)(2,1)S(1)}, bf16[10,1,512]{2,1,0:T(2,128)(2,1)S(1)}, u32[]{:S(2)}, u32[]{:S(2)}) %collective-permute-start.5) | collective-permute-done | bytes 10272 | tf_op jit(solution)/shard_map/ppermute | solution.py:15
  81.5 4.8 %collective-permute-start.6 = (bf16[1,16,512]{2,1,0:T(8,128)(2,1)S(1)}, bf16[1,16,512]{2,1,0:T(8,128)(2,1)S(1)}, u32[]{:S(2)}, u32[]{:S(2)}) collective-permute-start(bf16[1,16,512]{2,1,0:T(8,128)(2,1)S(1)} %get-tuple-element.238), channel_id=1, source_target_pairs={{0,4},{4,8},{8,12},{1,5},{5,9},{9,13},{2,6},{6,10},{10,14},{3,7},{... | collective-permute-start | bytes 49160 | tf_op jit(solution)/shard_map/ppermute | solution.py:12
  89.1 4.5 %collective-permute-start.9 = (bf16[10,1,512]{2,1,0:T(2,128)(2,1)S(1)}, bf16[10,1,512]{2,1,0:T(2,128)(2,1)S(1)}, u32[]{:S(2)}, u32[]{:S(2)}) collective-permute-start(bf16[10,1,512]{2,1,0:T(2,128)(2,1)S(1)} %get-tuple-element.233), channel_id=1, source_target_pairs={{0,2},{1,3},{4,6},{5,7},{8,10},{9,11},{12,14},{13,15},{16,18},{17,... | collective-permute-start | bytes 30728 | tf_op jit(solution)/shard_map/ppermute | solution.py:12
  93.7 1.5 collective-permute-done.9
  95.5 16.0 %all_gather.15 = bf16[32,16,512]{2,1,0:T(8,128)(2,1)S(1)} all-gather(bf16[8,16,512]{2,1,0:T(8,128)(2,1)S(1)} %fusion.44), channel_id=1, replica_groups=mesh['groups'=2,'tile'=4,'col'=2,'rep'=2] {'tile'}, dimensions={0}, use_global_device_ids=true | all-gather | bytes 655360 | tf_op jit(solution)/shard_map/all_gather | solution.py:132
  113.2 16.9 %while.25 = (s32[]{:T(128)}, bf16[5,576,64]{1,2,0:T(8,128)(2,1)S(1)}, s32[]{:T(128)}, bf16[5,32,1152]{2,1,0:T(8,128)(2,1)S(1)}, bf16[32,16,320]{2,1,0:T(8,128)(2...) while((s32[]{:T(128)}, ...), condition=%wide.region_15.16_spmd, body=%wide.region_14.15_spmd.sunk | while | flops 75825160 | bytes 4932813 | solution.py:155
  115.1 1.4 fusion.74
  118.3 1.4 fusion.74
  124.8 1.4 fusion.74
  128.1 1.4 fusion.74
  133.7 20.8 %all-gather.1 = f32[16,9,512]{2,1,0:T(8,128)S(1)} all-gather(f32[1,9,512]{2,1,0:T(8,128)S(1)} %bitcast.123), channel_id=2, replica_groups=mesh['groups'=2,'tile'=4,'col'=2,'rep'=2] {'tile','col','rep'}, dimensions={0}, use_global_device_ids=true | all-gather | bytes 313344 | tf_op jit(solution)/shard_map/all_gather | solution.py:122
  156.2 10.5 %all-reduce.5.cloned.1.call-done = (bf16[320,512]{1,0:T(8,128)(2,1)}, bf16[5,576,64]{1,2,0:T(8,128)(2,1)}) async-done(((bf16[320,512]{1,0:T(8,128)(2,1)}, bf16[5,576,64]{1,2,0:T(8,128)(2,1)}), (bf16[320,512]{1,0:T(8,128)(2,1)}, bf16[5,576,64]{1,2,0:T(8,128)(2,1)})) %all-reduce.5.cloned.1.call-update) | async-done | bytes 696336 | tf_op jit(solution)/shard_map/psum | solution.py:142
  166.7 1.9 convert_element_type.146
  168.5 1.9 convert_element_type.149
  170.5 58.2 %reduce-scatter.4.cloned.1.call-done = f32[32,512]{1,0:T(8,128)} async-done(((f32[512,512]{1,0:T(8,128)}), f32[32,512]{1,0:T(8,128)}) %reduce-scatter.4.cloned.1.call-update) | async-done | bytes 65552
  (130 shorter events, 42.3 us)
Async XLA Ops:
  7.2 71.9 %copy-start = (bf16[512,512]{1,0:T(8,128)(2,1)S(1)}, bf16[512,512]{1,0:T(8,128)(2,1)}, u32[]{:S(2)}) copy-start(bf16[512,512]{1,0:T(8,128)(2,1)} %param.16) | copy-start | bytes 1572868
  7.2 54.1 %all-gather.4.cloned.1.call-start = ((), (), s32[]{:S(2)}) async-start(), calls=%async_computation.2 | async-start | bytes 1638400 | tf_op jit(solution)/shard_map/all_gather | solution.py:44
  8.2 6.5 %collective-permute-start = (bf16[1,5,32,64]{3,2,1,0:T(8,128)(2,1)S(1)}, bf16[1,5,32,64]{3,2,1,0:T(8,128)(2,1)S(1)}, u32[]{:S(2)}, u32[]{:S(2)}) collective-permute-start(bf16[1,5,32,64]{3,2,1,0:T(8,128)(2,1)S(1)} %get-tuple-element.229), channel_id=1, source_target_pairs={{0,2},{1,3},{4,6},{5,7},{8,10},{9,11},{12,14},{13,15},{16,18},{17,... | collective-permute-start | bytes 61448 | tf_op jit(solution)/shard_map/ppermute | solution.py:12
  13.0 5.9 %collective-permute-start.1 = (bf16[1,5,32,64]{3,2,1,0:T(8,128)(2,1)S(1)}, bf16[1,5,32,64]{3,2,1,0:T(8,128)(2,1)S(1)}, u32[]{:S(2)}, u32[]{:S(2)}) collective-permute-start(bf16[1,5,32,64]{3,2,1,0:T(8,128)(2,1)S(1)} %get-tuple-element.228), channel_id=1, source_target_pairs={{2,0},{3,1},{6,4},{7,5},{10,8},{11,9},{14,12},{15,13},{18,16},{19,... | collective-permute-start | bytes 61448 | tf_op jit(solution)/shard_map/ppermute | solution.py:15
  14.4 152.3 %all-reduce.5.cloned.1.call-start = ((), (), s32[]{:S(2)}) async-start(), calls=%async_computation.4 | async-start | bytes 1474560 | tf_op jit(solution)/shard_map/psum | solution.py:142
  60.9 12.7 %copy-start.5 = (f32[9,512]{1,0:T(8,128)S(1)}, f32[9,512]{1,0:T(8,128)}, u32[]{:S(2)}) copy-start(f32[9,512]{1,0:T(8,128)} %param.15) | copy-start | bytes 55300
  63.0 16.1 %copy-start.4 = (bf16[1,8,16,512]{3,2,1,0:T(8,128)(2,1)S(1)}, bf16[1,8,16,512]{3,2,1,0:T(8,128)(2,1)}, u32[]{:S(2)}) copy-start(bf16[1,8,16,512]{3,2,1,0:T(8,128)(2,1)} %param.17) | copy-start | bytes 393220
  63.0 6.0 %collective-permute-start.3 = (bf16[1,16,512]{2,1,0:T(8,128)(2,1)S(1)}, bf16[1,16,512]{2,1,0:T(8,128)(2,1)S(1)}, u32[]{:S(2)}, u32[]{:S(2)}) collective-permute-start(bf16[1,16,512]{2,1,0:T(8,128)(2,1)S(1)} %get-tuple-element.241), channel_id=1, source_target_pairs={{4,0},{8,4},{12,8},{5,1},{9,5},{13,9},{6,2},{10,6},{14,10},{7,3},{... | collective-permute-start | bytes 49160 | tf_op jit(solution)/shard_map/ppermute | solution.py:15
  64.4 6.0 %collective-permute-start.2 = (bf16[1,16,512]{2,1,0:T(8,128)(2,1)S(1)}, bf16[1,16,512]{2,1,0:T(8,128)(2,1)S(1)}, u32[]{:S(2)}, u32[]{:S(2)}) collective-permute-start(bf16[1,16,512]{2,1,0:T(8,128)(2,1)S(1)} %get-tuple-element.240), channel_id=1, source_target_pairs={{0,4},{4,8},{8,12},{1,5},{5,9},{9,13},{2,6},{6,10},{10,14},{3,7},{... | collective-permute-start | bytes 49160 | tf_op jit(solution)/shard_map/ppermute | solution.py:12
  70.4 3.4 %collective-permute-start.4 = (bf16[10,1,512]{2,1,0:T(2,128)(2,1)S(1)}, bf16[10,1,512]{2,1,0:T(2,128)(2,1)S(1)}, u32[]{:S(2)}, u32[]{:S(2)}) collective-permute-start(bf16[10,1,512]{2,1,0:T(2,128)(2,1)S(1)} %get-tuple-element.236), channel_id=1, source_target_pairs={{0,2},{1,3},{4,6},{5,7},{8,10},{9,11},{12,14},{13,15},{16,18},{17,... | collective-permute-start | bytes 30728 | tf_op jit(solution)/shard_map/ppermute | solution.py:12
  72.4 5.7 %collective-permute-start.5 = (bf16[10,1,512]{2,1,0:T(2,128)(2,1)S(1)}, bf16[10,1,512]{2,1,0:T(2,128)(2,1)S(1)}, u32[]{:S(2)}, u32[]{:S(2)}) collective-permute-start(bf16[10,1,512]{2,1,0:T(2,128)(2,1)S(1)} %get-tuple-element.237), channel_id=1, source_target_pairs={{2,0},{3,1},{6,4},{7,5},{10,8},{11,9},{14,12},{15,13},{18,16},{19,... | collective-permute-start | bytes 30728 | tf_op jit(solution)/shard_map/ppermute | solution.py:15
  80.2 6.1 %collective-permute-start.7 = (bf16[1,16,512]{2,1,0:T(8,128)(2,1)S(1)}, bf16[1,16,512]{2,1,0:T(8,128)(2,1)S(1)}, u32[]{:S(2)}, u32[]{:S(2)}) collective-permute-start(bf16[1,16,512]{2,1,0:T(8,128)(2,1)S(1)} %get-tuple-element.239), channel_id=1, source_target_pairs={{4,0},{8,4},{12,8},{5,1},{9,5},{13,9},{6,2},{10,6},{14,10},{7,3},{... | collective-permute-start | bytes 49160 | tf_op jit(solution)/shard_map/ppermute | solution.py:15
  81.5 6.3 %collective-permute-start.6 = (bf16[1,16,512]{2,1,0:T(8,128)(2,1)S(1)}, bf16[1,16,512]{2,1,0:T(8,128)(2,1)S(1)}, u32[]{:S(2)}, u32[]{:S(2)}) collective-permute-start(bf16[1,16,512]{2,1,0:T(8,128)(2,1)S(1)} %get-tuple-element.238), channel_id=1, source_target_pairs={{0,4},{4,8},{8,12},{1,5},{5,9},{9,13},{2,6},{6,10},{10,14},{3,7},{... | collective-permute-start | bytes 49160 | tf_op jit(solution)/shard_map/ppermute | solution.py:12
  87.8 5.9 %collective-permute-start.8 = (bf16[10,1,512]{2,1,0:T(2,128)(2,1)S(1)}, bf16[10,1,512]{2,1,0:T(2,128)(2,1)S(1)}, u32[]{:S(2)}, u32[]{:S(2)}) collective-permute-start(bf16[10,1,512]{2,1,0:T(2,128)(2,1)S(1)} %get-tuple-element.232), channel_id=1, source_target_pairs={{2,0},{3,1},{6,4},{7,5},{10,8},{11,9},{14,12},{15,13},{18,16},{19,... | collective-permute-start | bytes 30728 | tf_op jit(solution)/shard_map/ppermute | solution.py:15
  89.1 6.0 %collective-permute-start.9 = (bf16[10,1,512]{2,1,0:T(2,128)(2,1)S(1)}, bf16[10,1,512]{2,1,0:T(2,128)(2,1)S(1)}, u32[]{:S(2)}, u32[]{:S(2)}) collective-permute-start(bf16[10,1,512]{2,1,0:T(2,128)(2,1)S(1)} %get-tuple-element.233), channel_id=1, source_target_pairs={{0,2},{1,3},{4,6},{5,7},{8,10},{9,11},{12,14},{13,15},{16,18},{17,... | collective-permute-start | bytes 30728 | tf_op jit(solution)/shard_map/ppermute | solution.py:12
  111.5 1.1 copy-start.2
  130.2 0.8 copy-start.1
  131.0 97.7 %reduce-scatter.4.cloned.1.call-start = ((), (), s32[]{:S(2)}) async-start(), calls=%async_computation.3 | async-start | bytes 1114112
  132.3 1.4 copy-start.6
  132.3 1.4 copy-start.7
  132.3 1.4 copy-start.8
  133.6 21.6 %copy-start.3 = (bf16[8,16,512]{2,1,0:T(8,128)(2,1)S(1)}, bf16[8,16,512]{2,1,0:T(8,128)(2,1)}, u32[]{:S(2)}) copy-start(bf16[8,16,512]{2,1,0:T(8,128)(2,1)} %get-tuple-element.208) | copy-start | bytes 393220
Sparse Core Ops, SparseCore 0:
  14.5 34.9 all-gather.3
  131.1 35.5 all-reduce.4
  170.9 57.8 reduce-scatter.3
